TPU v7x, 32 devices: a whole 2x2x4 slice. The times are simulated.
32 devices in a mesh: groups: 2 (over y), epoch: 4 (over z), strip: 2 (over x), band: 2 (over core).
Axes of the slice: x: 2, y: 2, z: 4, core: 2. Of those that a mesh axis runs over, the one named last changes fastest.
Arguments:
- template: bfloat16 [16, 48, 512], P(('groups', 'epoch'), 'strip', 'band'), parts along dimension 0, may hold values from -6 to 6
- science: float32 [32, 48, 512], P(('groups', 'epoch'), 'strip', 'band'), parts along dimension 0, may hold values from -6 to 6
- variance: float32 [32, 48, 512], P(('groups', 'epoch'), 'strip', 'band'), parts along dimension 0, may hold values from 2 to 40
- bad_mask: int32 [32, 48, 512], P(('groups', 'epoch'), 'strip', 'band'), parts along dimension 0, may hold values 0 or 1
- intersection: int32 [32], P('groups'), parts along dimension 0, may hold values from 0 to 7, as said below
- offsets: int32 [32, 2], P(('groups', 'epoch')), parts along dimension 0, may hold values from -4 to 4
- basis_index: int32 [32, 16], P(('groups', 'epoch')), parts along dimension 0, may hold values from 0 to 48
- coefficients: float32 [32, 16, 6], P(('groups', 'epoch')), parts along dimension 0, may hold values from -2 to 2
- basis: float32 [49, 19, 19], replicated, may hold values from -0.3125 to 0.3125
Outputs:
- residual_image: float32 [32, 48, 512], P(('groups', 'epoch'), 'strip', 'band'), parts along dimension 0
- coadd: float32 [16, 48, 512], P(('groups', 'epoch'), 'strip', 'band'), parts along dimension 0
There are 2 independent parts, one for each index of `groups`. A program takes and returns all parts, laid end to end along the dimension named above; an argument that names none is the same for every part. Nothing has to cross between parts.
Inputs may be any that keep to these rules, and one draw needn't show every extreme that they name: `intersection`: exposure d * 4 + k (k < 4) covers a tile with index from (k) * 2 to (k) * 2 + 1, chosen at random among these.
All inputs are finite; a program needn't handle non-finite values. No bound on the sum of `bad_mask` on one device may be relied on, other than what follows from the above.
Results may differ from a plain program's by a relative error of at most 0.0018.
Values may be sent and summed in bfloat16 or wider, within the bound.
A program may use at most 64 MiB of HBM per device.

v0:
```python
import jax
import jax.numpy as jnp
from jax import lax
from jax.sharding import PartitionSpec as P

KS = 19
HALF = 9
SHIFT = 4
NPOLY = 6


highest = lax.Precision.HIGHEST


def padded_2(block, sides, width):
    for axis, dim in sides:
        count = lax.axis_size(axis)
        forward = [(i, i + 1) for i in range(count - 1)]
        backward = [(target, source) for source, target in forward]
        low = lax.ppermute(
            lax.slice_in_dim(block, block.shape[dim] - width, None, axis=dim), axis, forward
        )
        high = lax.ppermute(lax.slice_in_dim(block, 0, width, axis=dim), axis, backward)
        block = jnp.concatenate([low, block, high], axis=dim)
    return block


def poly_terms(rows_unit, cols_unit):
    ones = jnp.ones_like(rows_unit * cols_unit)
    return jnp.stack(
        [
            ones,
            rows_unit * ones,
            cols_unit * ones,
            rows_unit * rows_unit * ones,
            rows_unit * cols_unit,
            cols_unit * cols_unit * ones,
        ]
    )


def local(
    template, science, variance, bad_mask, intersection, offsets, basis_index, coefficients, basis
):
    n_epoch = lax.axis_size("epoch")
    my_index = lax.axis_index("epoch")
    tile_dev = template.shape[0]
    exp_dev, height, width = science.shape
    per_owner = exp_dev // n_epoch
    table = intersection.reshape(n_epoch, n_epoch, per_owner)
    wanted = lax.dynamic_index_in_dim(table, my_index, 1, keepdims=False)
    local_ids = jnp.clip(wanted - my_index * tile_dev, 0, tile_dev - 1).reshape(-1)
    my_tiles = lax.dynamic_slice_in_dim(intersection, my_index * exp_dev, exp_dev)
    piece = lax.all_gather(template, "epoch", axis=0, tiled=True)
    count = piece.shape[0]
    inside = (my_tiles >= 0) & (my_tiles < count)
    chosen = jnp.take(piece, jnp.clip(my_tiles, 0, count - 1), axis=0)
    arrived = jnp.where(
        inside[:, None, None], chosen, jnp.zeros((exp_dev, height, width), jnp.bfloat16)
    )
    padded = padded_2(arrived, (("strip", 1), ("band", 2)), HALF + SHIFT)
    picked = jnp.take(basis, basis_index, axis=0)
    kernels = jnp.einsum("ejp,ejab->epab", coefficients, picked, precision=highest).astype(
        jnp.bfloat16
    )
    span = height + 2 * HALF
    distance = jnp.arange(span)[None, :] - jnp.arange(height)[:, None]
    selector = (distance[None] == jnp.arange(KS)[:, None, None]).astype(jnp.bfloat16)
    row_global = lax.axis_index("strip") * height + jnp.arange(height)
    col_global = lax.axis_index("band") * width + jnp.arange(width)
    rows_unit = (2.0 * row_global.astype(jnp.float32) + 1.0) / (
        height * lax.axis_size("strip")
    ) - 1.0
    cols_unit = (2.0 * col_global.astype(jnp.float32) + 1.0) / (width * lax.axis_size("band")) - 1.0
    shapes = poly_terms(rows_unit[:, None], cols_unit[None, :])

    def one_model(item):
        slab, shift, kernel = item
        window = lax.dynamic_slice(
            slab, (SHIFT + shift[0], SHIFT + shift[1]), (span, width + 2 * HALF)
        )
        stacked = jnp.concatenate(
            [window[:, column : column + width] for column in range(KS)], axis=0
        )
        toeplitz = jnp.einsum("pij,iyz->pyjz", kernel, selector, preferred_element_type=jnp.float32)
        toeplitz = toeplitz.astype(jnp.bfloat16).reshape(NPOLY * height, KS * span)
        conv = jnp.dot(toeplitz, stacked, preferred_element_type=jnp.float32).reshape(
            NPOLY, height, width
        )
        return jnp.sum(conv * shapes, axis=0)

    models = lax.map(one_model, (padded, offsets, kernels))
    residual_image = science - models
    weight = bad_mask.astype(jnp.float32) / variance
    weighted = weight * residual_image
    numer_back, denom_back = (
        lax.all_to_all(
            weighted.reshape(n_epoch, per_owner, height, width),
            "epoch",
            split_axis=0,
            concat_axis=0,
            tiled=True,
        ),
        lax.all_to_all(
            weight.reshape(n_epoch, per_owner, height, width),
            "epoch",
            split_axis=0,
            concat_axis=0,
            tiled=True,
        ),
    )
    onehot = (local_ids[:, None] == jnp.arange(tile_dev)[None, :]).astype(jnp.float32)
    numer = jnp.einsum(
        "st,shw->thw", onehot, numer_back.reshape(-1, height, width), precision=highest
    )
    denom = jnp.einsum(
        "st,shw->thw", onehot, denom_back.reshape(-1, height, width), precision=highest
    )
    return (residual_image, numer / (denom + 1.0))


def solution(mesh):
    in_specs = (
        P(("groups", "epoch"), "strip", "band"),
        P(("groups", "epoch"), "strip", "band"),
        P(("groups", "epoch"), "strip", "band"),
        P(("groups", "epoch"), "strip", "band"),
        P("groups"),
        P(("groups", "epoch"), None),
        P(("groups", "epoch"), None),
        P(("groups", "epoch"), None, None),
        P(),
    )
    out_specs = (P(("groups", "epoch"), "strip", "band"), P(("groups", "epoch"), "strip", "band"))
    return jax.shard_map(local, mesh=mesh, in_specs=in_specs, out_specs=out_specs, check_vma=False)
```

profile of v0, /device:TPU:0, one launch (start us, length us, event | category | flops | bytes accessed | tf_op | source)
XLA Modules:
  0.0 87.0 jit_solution(12005535667029276163)
XLA Ops:
  0.6 15.3 %all_gather.3 = bf16[8,24,256]{2,1,0:T(8,128)(2,1)S(1)} all-gather(bf16[2,24,256]{2,1,0:T(8,128)(2,1)} %param.11), channel_id=1, replica_groups=mesh['groups'=2,'epoch'=4,'strip'=2,'band'=2] {'epoch'}, dimensions={0}, use_global_device_ids=true | all-gather | bytes 122880 | tf_op jit(solution)/shard_map/all_gather | solution.py:54
  15.9 0.7 compare_and_fusion
  17.3 1.3 %collective-permute-start.1 = (bf16[4,13,256]{2,1,0:T(8,128)(2,1)S(1)}, bf16[4,13,256]{2,1,0:T(8,128)(2,1)S(1)}, u32[]{:S(2)}, u32[]{:S(2)}) collective-permute-start(bf16[4,13,256]{2,1,0:T(8,128)(2,1)S(1)} %get-tuple-element.206), channel_id=1, source_target_pairs={{2,0},{3,1},{6,4},{7,5},{10,8},{11,9},{14,12},{15,13},{18,16},{19,... | collective-permute-start | bytes 79880 | tf_op jit(solution)/shard_map/ppermute | solution.py:23
  18.6 4.5 %collective-permute-start = (bf16[4,13,256]{2,1,0:T(8,128)(2,1)S(1)}, bf16[4,13,256]{2,1,0:T(8,128)(2,1)S(1)}, u32[]{:S(2)}, u32[]{:S(2)}) collective-permute-start(bf16[4,13,256]{2,1,0:T(8,128)(2,1)S(1)} %get-tuple-element.205), channel_id=1, source_target_pairs={{0,2},{1,3},{4,6},{5,7},{8,10},{9,11},{12,14},{13,15},{16,18},{17,... | collective-permute-start | bytes 79880 | tf_op jit(solution)/shard_map/ppermute | solution.py:20
  23.2 0.7 compare_select_fusion
  23.9 0.7 compare_and_fusion.2
  24.6 1.3 %copy.31 = f32[49,19,19]{2,1,0:T(8,128)S(1)} copy(f32[49,19,19]{0,2,1:T(8,128)} %param.19) | data formatting | bytes 141512 | tf_op args[8]
  26.0 0.6 gather_fusion
  26.6 0.6 copy.42
  27.6 4.5 %fusion.12 = bf16[4,6,19,19]{3,1,2,0:T(8,128)(2,1)S(1)} fusion(f32[4,16,19,19]{1,0,3,2:T(4,128)S(1)} %broadcast_select_fusion, f32[4,16,6,1]{1,0,2,3:T(4,128)S(1)} %bitcast.66), kind=kOutput, calls=%fused_computation.19 | convolution fusion | flops 1672152 | bytes 111280 | tf_op jit(solution)/shard_map/ejp,ejab->epab/dot_general | solution.py:63
  32.3 1.3 %collective-permute-start.3 = (bf16[4,50,13]{2,1,0:T(8,128)(2,1)S(1)}, bf16[4,50,13]{2,1,0:T(8,128)(2,1)S(1)}, u32[]{:S(2)}, u32[]{:S(2)}) collective-permute-start(bf16[4,50,13]{2,1,0:T(8,128)(2,1)S(1)} %get-tuple-element.204), channel_id=1, source_target_pairs={{1,0},{3,2},{5,4},{7,6},{9,8},{11,10},{13,12},{15,14},{17,16},{19,... | collective-permute-start | bytes 15608 | tf_op jit(solution)/shard_map/ppermute | solution.py:23
  33.6 3.0 %collective-permute-start.2 = (bf16[4,50,13]{2,1,0:T(8,128)(2,1)S(1)}, bf16[4,50,13]{2,1,0:T(8,128)(2,1)S(1)}, u32[]{:S(2)}, u32[]{:S(2)}) collective-permute-start(bf16[4,50,13]{2,1,0:T(8,128)(2,1)S(1)} %get-tuple-element.203), channel_id=1, source_target_pairs={{0,1},{2,3},{4,5},{6,7},{8,9},{10,11},{12,13},{14,15},{16,17},{18,... | collective-permute-start | bytes 15608 | tf_op jit(solution)/shard_map/ppermute | solution.py:20
  36.9 0.6 collective-permute-done.2
  37.7 27.8 %while.14 = (s32[]{:T(128)}, f32[4,24,256]{2,1,0:T(8,128)S(1)}, bf16[4,6,19,19]{2,3,1,0:T(8,128)(2,1)S(1)}, s32[4,2]{0,1:T(2,128)S(1)}, bf16[4,50,282]{2,1,0:T(8...) while((s32[]{:T(128)}, f32[4,24,256]{2,1,0:T(8,128)S(1)}, ...), condition=%wide.region_2.3_spmd.clone, body=%wide.region_0.2_spmd.clone.sunk | while | flops 63422412 | bytes 3278881 | solution.py:92
  42.0 2.3 %concatenate.17 = bf16[798,256]{1,0:T(8,128)(2,1)S(1)} concatenate(bf16[42,256]{1,0:T(8,128)(2,1)S(1)} %get-tuple-element.276, bf16[42,256]{1,0:T(8,128)(2,1)S(1)} %get-tuple-element.277, bf16[42,256]{1,0:T(8,128)(2,1)S(1)} %get-tuple-element.278, bf16[42,256]{1,0:T(8,128)(2,1)S(1)} %get-tuple-element.279, bf16[42,256]{1,0:T(8,128)(2,1)S(1)} %get-tuple-element.280, ...), dimensions={0} | concatenate | bytes 817152 | tf_op jit(solution)/shard_map/while/body/eval_jaxpr/concatenate | solution.py:82
  49.0 2.3 %concatenate.17 = bf16[798,256]{1,0:T(8,128)(2,1)S(1)} concatenate(bf16[42,256]{1,0:T(8,128)(2,1)S(1)} %get-tuple-element.276, bf16[42,256]{1,0:T(8,128)(2,1)S(1)} %get-tuple-element.277, bf16[42,256]{1,0:T(8,128)(2,1)S(1)} %get-tuple-element.278, bf16[42,256]{1,0:T(8,128)(2,1)S(1)} %get-tuple-element.279, bf16[42,256]{1,0:T(8,128)(2,1)S(1)} %get-tuple-element.280, ...), dimensions={0} | concatenate | bytes 817152 | tf_op jit(solution)/shard_map/while/body/eval_jaxpr/concatenate | solution.py:82
  56.0 2.3 %concatenate.17 = bf16[798,256]{1,0:T(8,128)(2,1)S(1)} concatenate(bf16[42,256]{1,0:T(8,128)(2,1)S(1)} %get-tuple-element.276, bf16[42,256]{1,0:T(8,128)(2,1)S(1)} %get-tuple-element.277, bf16[42,256]{1,0:T(8,128)(2,1)S(1)} %get-tuple-element.278, bf16[42,256]{1,0:T(8,128)(2,1)S(1)} %get-tuple-element.279, bf16[42,256]{1,0:T(8,128)(2,1)S(1)} %get-tuple-element.280, ...), dimensions={0} | concatenate | bytes 817152 | tf_op jit(solution)/shard_map/while/body/eval_jaxpr/concatenate | solution.py:82
  62.9 2.3 %concatenate.17 = bf16[798,256]{1,0:T(8,128)(2,1)S(1)} concatenate(bf16[42,256]{1,0:T(8,128)(2,1)S(1)} %get-tuple-element.276, bf16[42,256]{1,0:T(8,128)(2,1)S(1)} %get-tuple-element.277, bf16[42,256]{1,0:T(8,128)(2,1)S(1)} %get-tuple-element.278, bf16[42,256]{1,0:T(8,128)(2,1)S(1)} %get-tuple-element.279, bf16[42,256]{1,0:T(8,128)(2,1)S(1)} %get-tuple-element.280, ...), dimensions={0} | concatenate | bytes 817152 | tf_op jit(solution)/shard_map/while/body/eval_jaxpr/concatenate | solution.py:82
  65.6 0.7 multiply_bitcast_fusion
  66.3 4.7 %all-to-all-start = ((f32[4,1,24,256]{3,2,1,0:T(8,128)}), f32[4,1,24,256]{3,2,1,0:T(8,128)S(1)}, u32[]{:S(2)}, u32[]{:S(2)}) async-start(f32[4,1,24,256]{3,2,1,0:T(8,128)} %get-tuple-element.177), calls=%async_computation | async-start | bytes 196608 | tf_op jit(solution)/shard_map/all_to_all | solution.py:97
  71.3 5.7 %all-to-all-done = f32[4,1,24,256]{3,2,1,0:T(8,128)S(1)} async-done(((f32[4,1,24,256]{3,2,1,0:T(8,128)}), f32[4,1,24,256]{3,2,1,0:T(8,128)S(1)}, u32[]{:S(2)}, u32[]{:S(2)}) %all-to-all-start) | async-done | bytes 98336 | tf_op jit(solution)/shard_map/all_to_all | solution.py:97
  77.0 3.3 %all-to-all-start.1 = ((f32[4,1,24,256]{3,2,1,0:T(8,128)}), f32[4,1,24,256]{3,2,1,0:T(8,128)S(1)}, u32[]{:S(2)}, u32[]{:S(2)}) async-start(f32[4,1,24,256]{3,2,1,0:T(8,128)} %get-tuple-element.202), calls=%async_computation.1 | async-start | bytes 196608 | tf_op jit(solution)/shard_map/all_to_all | solution.py:104
  80.6 5.6 %all-to-all-done.1 = f32[4,1,24,256]{3,2,1,0:T(8,128)S(1)} async-done(((f32[4,1,24,256]{3,2,1,0:T(8,128)}), f32[4,1,24,256]{3,2,1,0:T(8,128)S(1)}, u32[]{:S(2)}, u32[]{:S(2)}) %all-to-all-start.1) | async-done | bytes 98336 | tf_op jit(solution)/shard_map/all_to_all | solution.py:104
  86.4 0.6 copy.39
  (73 shorter events, 10.5 us)
Async XLA Ops:
  0.6 26.9 %copy-start = (f32[4,16,6]{1,0,2:T(4,128)S(1)}, f32[4,16,6]{1,0,2:T(4,128)}, u32[]{:S(2)}) copy-start(f32[4,16,6]{1,0,2:T(4,128)} %param.18) | copy-start | bytes 4612
  17.3 14.8 %collective-permute-start.1 = (bf16[4,13,256]{2,1,0:T(8,128)(2,1)S(1)}, bf16[4,13,256]{2,1,0:T(8,128)(2,1)S(1)}, u32[]{:S(2)}, u32[]{:S(2)}) collective-permute-start(bf16[4,13,256]{2,1,0:T(8,128)(2,1)S(1)} %get-tuple-element.206), channel_id=1, source_target_pairs={{2,0},{3,1},{6,4},{7,5},{10,8},{11,9},{14,12},{15,13},{18,16},{19,... | collective-permute-start | bytes 79880 | tf_op jit(solution)/shard_map/ppermute | solution.py:23
  18.6 13.5 %collective-permute-start = (bf16[4,13,256]{2,1,0:T(8,128)(2,1)S(1)}, bf16[4,13,256]{2,1,0:T(8,128)(2,1)S(1)}, u32[]{:S(2)}, u32[]{:S(2)}) collective-permute-start(bf16[4,13,256]{2,1,0:T(8,128)(2,1)S(1)} %get-tuple-element.205), channel_id=1, source_target_pairs={{0,2},{1,3},{4,6},{5,7},{8,10},{9,11},{12,14},{13,15},{16,18},{17,... | collective-permute-start | bytes 79880 | tf_op jit(solution)/shard_map/ppermute | solution.py:20
  27.6 10.1 %copy-start.4 = (s32[4,2]{0,1:T(2,128)S(1)}, s32[4,2]{0,1:T(2,128)}, u32[]{:S(2)}) copy-start(s32[4,2]{0,1:T(2,128)} %param.16) | copy-start | bytes 100
  32.3 4.6 %collective-permute-start.3 = (bf16[4,50,13]{2,1,0:T(8,128)(2,1)S(1)}, bf16[4,50,13]{2,1,0:T(8,128)(2,1)S(1)}, u32[]{:S(2)}, u32[]{:S(2)}) collective-permute-start(bf16[4,50,13]{2,1,0:T(8,128)(2,1)S(1)} %get-tuple-element.204), channel_id=1, source_target_pairs={{1,0},{3,2},{5,4},{7,6},{9,8},{11,10},{13,12},{15,14},{17,16},{19,... | collective-permute-start | bytes 15608 | tf_op jit(solution)/shard_map/ppermute | solution.py:23
  33.6 3.9 %collective-permute-start.2 = (bf16[4,50,13]{2,1,0:T(8,128)(2,1)S(1)}, bf16[4,50,13]{2,1,0:T(8,128)(2,1)S(1)}, u32[]{:S(2)}, u32[]{:S(2)}) collective-permute-start(bf16[4,50,13]{2,1,0:T(8,128)(2,1)S(1)} %get-tuple-element.203), channel_id=1, source_target_pairs={{0,1},{2,3},{4,5},{6,7},{8,9},{10,11},{12,13},{14,15},{16,17},{18,... | collective-permute-start | bytes 15608 | tf_op jit(solution)/shard_map/ppermute | solution.py:20
  37.7 27.9 %copy-start.1 = (f32[4,24,256]{2,1,0:T(8,128)S(1)}, f32[4,24,256]{2,1,0:T(8,128)}, u32[]{:S(2)}) copy-start(f32[4,24,256]{2,1,0:T(8,128)} %param.13) | copy-start | bytes 294916
  37.7 27.9 %copy-start.2 = (s32[4,24,256]{2,1,0:T(8,128)S(1)}, s32[4,24,256]{2,1,0:T(8,128)}, u32[]{:S(2)}) copy-start(s32[4,24,256]{2,1,0:T(8,128)} %param.14) | copy-start | bytes 294916
  37.7 27.9 %copy-start.3 = (f32[4,24,256]{2,1,0:T(8,128)S(1)}, f32[4,24,256]{2,1,0:T(8,128)}, u32[]{:S(2)}) copy-start(f32[4,24,256]{2,1,0:T(8,128)} %param.12) | copy-start | bytes 294916
  65.5 5.5 %copy-start.5 = (s32[16]{0:T(128)S(1)}, s32[16]{0:T(128)}, u32[]{:S(2)}) copy-start(s32[16]{0:T(128)} %param.15) | copy-start | bytes 196
  66.3 10.7 %all-to-all-start = ((f32[4,1,24,256]{3,2,1,0:T(8,128)}), f32[4,1,24,256]{3,2,1,0:T(8,128)S(1)}, u32[]{:S(2)}, u32[]{:S(2)}) async-start(f32[4,1,24,256]{3,2,1,0:T(8,128)} %get-tuple-element.177), calls=%async_computation | async-start | bytes 196608 | tf_op jit(solution)/shard_map/all_to_all | solution.py:97
  77.0 9.1 %all-to-all-start.1 = ((f32[4,1,24,256]{3,2,1,0:T(8,128)}), f32[4,1,24,256]{3,2,1,0:T(8,128)S(1)}, u32[]{:S(2)}, u32[]{:S(2)}) async-start(f32[4,1,24,256]{3,2,1,0:T(8,128)} %get-tuple-element.202), calls=%async_computation.1 | async-start | bytes 196608 | tf_op jit(solution)/shard_map/all_to_all | solution.py:104
where the time goes:
time: 87.7 us; the launch traced here: 87 us
  local copies, waits for them, and re-layouts  19.1 us (22%)
  starting transfers between devices  18.2 us (21%)
  blocking collectives  15.3 us (17%)
  waiting for transfers between devices  11.8 us (13%)
  loops' own time  10.6 us (12%)
  matrix products  7.48 us (9%)
  other arithmetic  3.59 us (4%)
  between operations  0.89 us (1%)
    all_gather x1, blocking collectives, local(): piece = lax.all_gather(template, 'epoch', axis=0, tiled=True)  15.3 us
    another operation x1, loops' own time, local(): models = lax.map(one_model, (padded, offsets, kernels))  10.6 us
    concatenate x4, local copies, waits for them, and re-layouts, one_model(): jnp.concatenate([window[:, column:column + width] for column in range(KS)...  9.31 us
    ppermute x2, starting transfers between devices, padded_2(): lax.ppermute(lax.slice_in_dim(block, block.shape[dim] - width, None, axis...  7.58 us
    all_to_all x1, waiting for transfers between devices, local(): lax.all_to_all(weighted.reshape(n_epoch, per_owner, height, width), 'epoc...  5.71 us
    all_to_all x1, waiting for transfers between devices, local(): lax.all_to_all(weight.reshape(n_epoch, per_owner, height, width), 'epoch'...  5.56 us
    all_to_all x1, starting transfers between devices, local(): lax.all_to_all(weighted.reshape(n_epoch, per_owner, height, width), 'epoc...  4.72 us
    dot_general x1, matrix products, local(): jnp.einsum('ejp,ejab->epab', coefficients, picked, precision=highest)  4.52 us
  transfers between devices with their start and end apart: 6, of which 3 were waited for; matrix products, arithmetic and copies ran while one was open for 11% of the time, Pallas kernels for 0%

commit v1 on v0

v1 whole, which is shorter than its diff:
```python
import functools

import jax
import jax.numpy as jnp
from jax import lax
from jax.experimental import pallas as pl
from jax.experimental.pallas import tpu as pltpu
from jax.sharding import PartitionSpec as P

HALF = 9
SHIFT = 4
RIM = HALF + SHIFT
EDGE_ROWS = 16
LANES = 128
SLOT = 64

MESH = pl.DeviceIdType.MESH
STEPS = [(ds, db) for ds in (0, -1, 1) for db in (0, -1, 1)]


def kernel(
    sizes,
    intersection,
    offsets,
    basis_index,
    coefficients,
    template,
    science,
    variance,
    bad_mask,
    basis,
    residual,
    coadd,
    full,
    bottom,
    mid,
    top,
    low,
    kernel_rows,
    pairs,
    turns,
    toeplitz,
    weight,
    weight_out,
    weight_in,
    value_out,
    value_in,
    own_value,
    send_sem,
    recv_sem,
    back_send,
    back_recv,
):
    n_epoch, n_strip, n_band = sizes
    tile_dev, height, width = template.shape
    exp_dev = science.shape[0]
    n_sel, n_poly = coefficients.shape[1:]
    ks = basis.shape[1]
    group = lax.axis_index("groups")
    me = lax.axis_index("epoch")
    strip = lax.axis_index("strip")
    band = lax.axis_index("band")

    def target(epoch, ds, db):
        return (group, epoch, strip + ds, band + db)

    def there(ds, db):
        sides = []
        if ds < 0:
            sides.append(strip >= -ds)
        if ds > 0:
            sides.append(strip < n_strip - ds)
        if db < 0:
            sides.append(band >= -db)
        if db > 0:
            sides.append(band < n_band - db)
        return sides

    def guarded(sides, body):
        if not sides:
            body()
        elif len(sides) == 1:
            pl.when(sides[0])(body)
        else:
            pl.when(jnp.logical_and(sides[0], sides[1]))(body)

    barrier = pltpu.get_barrier_semaphore()
    for ds, db in STEPS:

        def greet(ds=ds, db=db):
            for step in range(n_epoch):
                if step == 0 and ds == 0 and db == 0:
                    continue
                epoch = lax.rem(me + step, n_epoch)
                pl.semaphore_signal(
                    barrier, inc=1, device_id=target(epoch, ds, db), device_id_type=MESH
                )

        guarded(there(ds, db), greet)

    for step in range(n_epoch):
        epoch = lax.rem(me + step, n_epoch)
        tile = intersection[epoch * exp_dev + me] - me * tile_dev
        chosen = template[jnp.clip(tile, 0, tile_dev - 1)]
        full[epoch] = chosen
        wide = chosen.astype(jnp.float32)
        bottom[epoch] = wide[height - EDGE_ROWS :].astype(jnp.bfloat16)
    mid[me, :, LANES : LANES + width] = full[me]

    zero = jnp.bfloat16(0)

    @pl.when(strip == 0)
    def _():
        top[...] = jnp.full(top.shape, zero)

    @pl.when(strip == n_strip - 1)
    def _():
        low[...] = jnp.full(low.shape, zero)

    for edge, lanes in ((band == 0, slice(0, LANES)), (band == n_band - 1, slice(LANES + width, None))):

        @pl.when(edge)
        def _(lanes=lanes):
            mid[:, :, lanes] = jnp.full(mid[:, :, lanes].shape, zero)

            @pl.when(strip > 0)
            def _():
                top[:, :, lanes] = jnp.full(top[:, :, lanes].shape, zero)

            @pl.when(strip < n_strip - 1)
            def _():
                low[:, :, lanes] = jnp.full(low[:, :, lanes].shape, zero)

    for exposure in range(exp_dev):
        value = bad_mask[exposure].astype(jnp.float32) / variance[exposure]
        weight[exposure] = value
        weight_out[exposure] = value.astype(jnp.bfloat16)

    kernel_rows[...] = jnp.zeros(kernel_rows.shape, jnp.float32)

    def sum_kernels(exposure, carry):
        sums = [jnp.zeros((ks, ks), jnp.float32) for _ in range(n_poly)]
        for j in range(n_sel):
            image = basis[basis_index[exposure, j]]
            for p in range(n_poly):
                sums[p] = sums[p] + coefficients[exposure, j, p] * image
        for p in range(n_poly):
            kernel_rows[exposure, p * LANES : p * LANES + ks, 0:ks] = sums[p]
        return carry

    lax.fori_loop(0, exp_dev, sum_kernels, 0)

    partners = n_epoch
    if n_strip > 1:
        near = jnp.minimum(strip, 1) + jnp.minimum(n_strip - 1 - strip, 1)
        partners = partners * (1 + near)
    if n_band > 1:
        near = jnp.minimum(band, 1) + jnp.minimum(n_band - 1 - band, 1)
        partners = partners * (1 + near)
    pl.semaphore_wait(barrier, partners - 1)

    def piece(step, ds, db, arriving):
        other = lax.rem(me + step, n_epoch)
        held = {0: slice(0, width), 1: slice(width - LANES, width), -1: slice(0, LANES)}[db]
        lands = {
            0: slice(LANES, LANES + width),
            1: slice(0, LANES),
            -1: slice(LANES + width, 2 * LANES + width),
        }[db]
        slot = other if arriving else me
        source = full.at[other, :, held]
        dest = mid
        if ds == 1:
            source, dest = bottom.at[other, :, held], top
        if ds == -1:
            source, dest = full.at[other, 0:EDGE_ROWS, held], low
        return pltpu.make_async_remote_copy(
            src_ref=source,
            dst_ref=dest.at[slot, :, lands],
            send_sem=send_sem.at[other, ds + 1, db + 1],
            recv_sem=recv_sem.at[slot, ds + 1, db + 1],
            device_id=target(other, ds, db),
            device_id_type=MESH,
        )

    for step in list(range(1, n_epoch)) + [0]:
        for ds, db in STEPS:
            if step == 0 and ds == 0 and db == 0:
                continue
            guarded(there(ds, db), lambda step=step, ds=ds, db=db: piece(step, ds, db, False).start())

    def back(which, out, into, step, arriving):
        other = lax.rem(me + step, n_epoch)
        slot = other if arriving else me
        return pltpu.make_async_remote_copy(
            src_ref=out.at[other],
            dst_ref=into.at[slot],
            send_sem=back_send.at[which, other],
            recv_sem=back_recv.at[which, slot],
            device_id=target(other, 0, 0),
            device_id_type=MESH,
        )

    for step in range(1, n_epoch):
        back(0, weight_out, weight_in, step, False).start()

    n_pairs = (ks + 1) // 2
    rows_all = pairs.shape[0]
    row = lax.broadcasted_iota(jnp.int32, (32, LANES), 0)
    col = lax.broadcasted_iota(jnp.int32, (32, LANES), 1)
    pick = jnp.where(row < 16, 2 * row, 2 * (row - 16) + 1)
    pick = (pick == col).astype(jnp.bfloat16)

    def build(exposure, carry):
        rows = kernel_rows[exposure].astype(jnp.bfloat16)
        turned = lax.dot_general(
            pick, rows, (((1,), (1,)), ((), ())), preferred_element_type=jnp.float32
        )
        for p in range(n_poly):
            block = turned[:, p * LANES : (p + 1) * LANES]
            both = block[:16] + pltpu.roll(block[16:], SLOT, 1)
            pairs[p * n_pairs : (p + 1) * n_pairs, :] = both[:n_pairs]
        shift = offsets[exposure, 0] + (SHIFT + EDGE_ROWS - RIM)
        every = pairs[...]
        for y in range(height):
            turns[y * rows_all : (y + 1) * rows_all, :] = pltpu.roll(every, shift + y, 1)
        for p in range(0, n_poly, 2):
            for q in range(n_pairs):
                halves = [
                    turns[pl.ds((p + h) * n_pairs + q, height, stride=rows_all), :]
                    for h in range(2)
                ]
                toeplitz[
                    exposure, p * height : (p + 2) * height, q * LANES : (q + 1) * LANES
                ] = jnp.concatenate(halves, axis=0).astype(jnp.bfloat16)
        return carry

    lax.fori_loop(0, exp_dev, build, 0)

    row = lax.broadcasted_iota(jnp.int32, (height, 1), 0) + strip * height
    col = lax.broadcasted_iota(jnp.int32, (1, width), 1) + band * width
    r = (2.0 * row.astype(jnp.float32) + 1.0) / (height * n_strip) - 1.0
    c = (2.0 * col.astype(jnp.float32) + 1.0) / (width * n_band) - 1.0
    r = jnp.broadcast_to(r, (height, width))
    c = jnp.broadcast_to(c, (height, width))

    def arrive(step):
        for ds, db in STEPS:
            if ds == 0 and db == 0 and step == 0:
                continue
            guarded(
                there(-ds, -db),
                lambda ds=ds, db=db: piece(step, ds, db, True).wait_recv(),
            )

    for step in range(n_epoch):
        k = lax.rem(me + step, n_epoch)
        arrive(step)
        slab = jnp.concatenate(
            [
                top[k].astype(jnp.float32),
                mid[k].astype(jnp.float32),
                low[k].astype(jnp.float32),
                jnp.zeros((SLOT - height - 2 * EDGE_ROWS, width + 2 * LANES), jnp.float32),
            ],
            axis=0,
        )
        total = width + 2 * LANES
        slab = pltpu.roll(slab, total - (LANES - RIM + SHIFT) - offsets[k, 1], 1)
        slab = slab[:, : width + LANES].astype(jnp.bfloat16)
        conv = jnp.zeros((n_poly * height, width), jnp.float32)
        for first in range(0, ks, 4):
            columns = range(first, min(first + 4, ks))
            stacked = jnp.concatenate([slab[:, b : b + width] for b in columns], axis=0)
            conv = conv + jnp.dot(
                toeplitz[k, :, first * SLOT : (first + len(columns)) * SLOT],
                stacked,
                preferred_element_type=jnp.float32,
            )
        q = [conv[p * height : (p + 1) * height] for p in range(n_poly)]
        model = q[0] + r * (q[1] + r * q[3] + c * q[4]) + c * (q[2] + c * q[5])
        left = science[k] - model
        residual[k] = left
        value = weight[k] * left
        if step == 0:
            own_value[...] = value
        else:
            value_out[k] = value.astype(jnp.bfloat16)
            back(1, value_out, value_in, step, False).start()

    numer = [None] * tile_dev
    denom = [None] * tile_dev
    for step in range(n_epoch):
        k = lax.rem(me + step, n_epoch)
        tile = intersection[k * exp_dev + me] - me * tile_dev
        if step == 0:
            upper, under = own_value[...], weight[me]
        else:
            back(0, weight_out, weight_in, step, True).wait_recv()
            back(1, value_out, value_in, step, True).wait_recv()
            upper = value_in[k].astype(jnp.float32)
            under = weight_in[k].astype(jnp.float32)
        for t in range(tile_dev):
            here = (tile == t).astype(jnp.float32)
            numer[t] = upper * here if step == 0 else numer[t] + upper * here
            denom[t] = under * here if step == 0 else denom[t] + under * here
    for t in range(tile_dev):
        coadd[t] = numer[t] / (denom[t] + 1.0)

    for step in range(n_epoch):
        for ds, db in STEPS:
            if step == 0 and ds == 0 and db == 0:
                continue
            guarded(
                there(ds, db),
                lambda step=step, ds=ds, db=db: piece(step, ds, db, False).wait_send(),
            )
        if step > 0:
            back(0, weight_out, weight_in, step, False).wait_send()
            back(1, value_out, value_in, step, False).wait_send()


def local(sizes, template, science, variance, bad_mask, intersection, offsets, basis_index, coefficients, basis):
    n_epoch = sizes[0]
    tile_dev, height, width = template.shape
    exp_dev = science.shape[0]
    assert exp_dev == n_epoch
    n_poly = coefficients.shape[2]
    ks = basis.shape[1]
    lanes_all = width + 2 * LANES
    n_pairs = (ks + 1) // 2
    rows_all = -(-n_poly * n_pairs // 8) * 8
    smem = pl.BlockSpec(memory_space=pltpu.SMEM)
    vmem = pl.BlockSpec(memory_space=pltpu.VMEM)
    bf16, f32 = jnp.bfloat16, jnp.float32
    dma = pltpu.SemaphoreType.DMA
    return pl.pallas_call(
        functools.partial(kernel, sizes),
        out_shape=(
            jax.ShapeDtypeStruct(science.shape, f32),
            jax.ShapeDtypeStruct(template.shape, f32),
        ),
        in_specs=[smem] * 4 + [vmem] * 5,
        out_specs=(vmem, vmem),
        scratch_shapes=[
            pltpu.VMEM((n_epoch, height, width), bf16),
            pltpu.VMEM((n_epoch, EDGE_ROWS, width), bf16),
            pltpu.VMEM((exp_dev, height, lanes_all), bf16),
            pltpu.VMEM((exp_dev, EDGE_ROWS, lanes_all), bf16),
            pltpu.VMEM((exp_dev, EDGE_ROWS, lanes_all), bf16),
            pltpu.VMEM((exp_dev, n_poly * LANES, LANES), f32),
            pltpu.VMEM((rows_all, LANES), f32),
            pltpu.VMEM((height * rows_all, LANES), f32),
            pltpu.VMEM((exp_dev, n_poly * height, n_pairs * LANES), bf16),
            pltpu.VMEM((exp_dev, height, width), f32),
            pltpu.VMEM((exp_dev, height, width), bf16),
            pltpu.VMEM((exp_dev, height, width), bf16),
            pltpu.VMEM((exp_dev, height, width), bf16),
            pltpu.VMEM((exp_dev, height, width), bf16),
            pltpu.VMEM((height, width), f32),
            dma((n_epoch, 3, 3)),
            dma((n_epoch, 3, 3)),
            dma((2, n_epoch)),
            dma((2, n_epoch)),
        ],
        compiler_params=pltpu.CompilerParams(collective_id=0, has_side_effects=True),
    )(
        intersection, offsets, basis_index, coefficients,
        template, science, variance, bad_mask, basis,
    )


def solution(mesh):
    sizes = (mesh.shape["epoch"], mesh.shape["strip"], mesh.shape["band"])
    image = P(("groups", "epoch"), "strip", "band")
    split = ("groups", "epoch")
    in_specs = (
        image, image, image, image, P("groups"),
        P(split, None), P(split, None), P(split, None, None), P(),
    )
    return jax.shard_map(
        functools.partial(local, sizes),
        mesh=mesh,
        in_specs=in_specs,
        out_specs=(image, image),
        check_vma=False,
    )
```

time: 87.7 us -> 26.5 us (0.30)
  Pallas kernels: 0 us -> 18.5 us
  starting transfers between devices: 18.2 us -> 0 us
  blocking collectives: 15.3 us -> 0 us
  local copies, waits for them, and re-layouts: 19.1 us -> 7 us
  waiting for transfers between devices: 11.8 us -> 0 us
  loops' own time: 10.6 us -> 0 us
  matrix products: 7.48 us -> 0 us
  other arithmetic: 3.59 us -> 0 us
    pallas_call x0 -> x1, Pallas kernels: none -> 18.5 us  [local(): pl.pallas_call(functools.partial(kernel, sizes), out_shape=(jax.ShapeDtyp...]
    all_gather x1 -> x0, blocking collectives: 15.3 us -> none  [local(): piece = lax.all_gather(template, 'epoch', axis=0, tiled=True)]
    all_to_all x2 -> x0, waiting for transfers between devices: 11.3 us -> none  [the longest x1 5.71 us: local(): lax.all_to_all(weighted.reshape(n_epoch, per_owner, height, width), 'epoc...]
    another operation x1 -> x0, loops' own time: 10.6 us -> none  [local(): models = lax.map(one_model, (padded, offsets, kernels))]
    ppermute x4 -> x0, starting transfers between devices: 10.2 us -> none  [the longest x2 7.58 us: padded_2(): lax.ppermute(lax.slice_in_dim(block, block.shape[dim] - width, None, axis...]
    concatenate x4 -> x0, local copies, waits for them, and re-layouts: 9.31 us -> none  [one_model(): jnp.concatenate([window[:, column:column + width] for column in range(KS)...]
    all_to_all x2 -> x0, starting transfers between devices: 8.03 us -> none  [the longest x1 4.72 us: local(): lax.all_to_all(weighted.reshape(n_epoch, per_owner, height, width), 'epoc...]
    dot_general x11 -> x0, matrix products: 7.48 us -> none  [the longest x1 4.52 us: local(): jnp.einsum('ejp,ejab->epab', coefficients, picked, precision=highest)]
  transfers between devices with their start and end apart: 6 -> 0, of which waited for: 3 -> 0; matrix products, arithmetic and copies ran while one was open for 11% -> 0% of each run, Pallas kernels for 0% -> 0%
where the time goes in v1:
time: 26.5 us; the launch traced here: 26.2 us
  Pallas kernels  18.5 us (70%)
  local copies, waits for them, and re-layouts  7 us (26%)
  between operations  0.65 us (2%)
    pallas_call x1, Pallas kernels, local(): pl.pallas_call(functools.partial(kernel, sizes), out_shape=(jax.ShapeDtyp...  18.5 us
    unnamed x7, local copies, waits for them, and re-layouts  7 us

profile of v1, /device:TPU:0, one launch (start us, length us, event | category | flops | bytes accessed | tf_op | source)
XLA Modules:
  0.0 26.2 jit_solution(13745612278558904306)
XLA Ops:
  0.6 1.3 %copy.11.offsets = s32[4,2]{1,0:T(4,128)} copy(s32[4,2]{0,1:T(2,128)} %param.14) | data formatting | bytes 64 | tf_op args[5]
  2.0 1.4 %copy.12.coefficients = f32[4,16,6]{2,1,0:T(8,128)} copy(f32[4,16,6]{1,0,2:T(4,128)} %param.16) | data formatting | bytes 3072 | tf_op args[7]
  3.4 2.1 %copy.13.basis = f32[49,19,19]{2,1,0:T(8,128)} copy(f32[49,19,19]{0,2,1:T(8,128)} %param.17) | data formatting | bytes 141512 | tf_op args[8]
  5.5 18.5 %shard_map.104 = (f32[4,24,256]{2,1,0:T(8,128)}, f32[2,24,256]{2,1,0:T(8,128)}) custom-call(s32[16]{0:T(128)} %intersection.1, s32[4,2]{1,0:T(4,128)} %copy.11.offsets, s32[4,16]{1,0:T(4,128)} %basis_index.1, f32[4,16,6]{2,1,0:T(8,128)} %copy.12.coefficients, bf16[2,24,256]{2,1,0:T(8,128)(2,1)} %template.1, f32[4,24,256]{2,1,0:T(8,128)} %science.1, ...), custom_call_target="tpu_custom_call" | custom-call | tf_op jit(solution)/shard_map/pallas_call | solution.py:337
  24.0 0.0 copy-start
  24.0 1.6 %copy.16 = f32[4,24,256]{2,1,0:T(8,128)} copy(f32[4,24,256]{2,1,0:T(8,128)} %get-tuple-element.4) | data formatting | bytes 196608
  25.6 0.0 copy-done
  25.6 0.6 %copy.17 = f32[2,24,256]{2,1,0:T(8,128)} copy(f32[2,24,256]{2,1,0:T(8,128)S(1)} %copy-done) | data formatting | bytes 98304
Async XLA Ops:
  24.0 1.6 %copy-start = (f32[2,24,256]{2,1,0:T(8,128)S(1)}, f32[2,24,256]{2,1,0:T(8,128)}, u32[]{:S(2)}) copy-start(f32[2,24,256]{2,1,0:T(8,128)} %get-tuple-element.5) | copy-start | bytes 147460

commit v2 on v1

--- a/solution.py
+++ b/solution.py
@@ -25,6 +25,12 @@
     basis_index,
     coefficients,
     template,
+    science_hbm,
+    variance_hbm,
+    bad_mask_hbm,
+    basis_hbm,
+    residual_out,
+    coadd_out,
     science,
     variance,
     bad_mask,
@@ -36,16 +42,16 @@
     mid,
     top,
     low,
-    kernel_rows,
+    turned_basis,
     pairs,
     turns,
     toeplitz,
     weight,
-    weight_out,
     weight_in,
     value_out,
     value_in,
     own_value,
+    local_sem,
     send_sem,
     recv_sem,
     back_send,
@@ -54,8 +60,8 @@
     n_epoch, n_strip, n_band = sizes
     tile_dev, height, width = template.shape
     exp_dev = science.shape[0]
-    n_sel, n_poly = coefficients.shape[1:]
-    ks = basis.shape[1]
+    n_poly, _, n_sel = coefficients.shape
+    ks, _, n_basis = basis.shape
     group = lax.axis_index("groups")
     me = lax.axis_index("epoch")
     strip = lax.axis_index("strip")
@@ -98,6 +104,20 @@
 
         guarded(there(ds, db), greet)
 
+    loads = [
+        pltpu.make_async_copy(held, here, local_sem.at[i])
+        for i, (held, here) in enumerate(
+            (
+                (basis_hbm, basis),
+                (variance_hbm, variance),
+                (bad_mask_hbm, bad_mask),
+                (science_hbm, science),
+            )
+        )
+    ]
+    for load in loads:
+        load.start()
+
     for step in range(n_epoch):
         epoch = lax.rem(me + step, n_epoch)
         tile = intersection[epoch * exp_dev + me] - me * tile_dev
@@ -131,24 +151,45 @@
             def _():
                 low[:, :, lanes] = jnp.full(low[:, :, lanes].shape, zero)
 
+    lane = lax.broadcasted_iota(jnp.int32, (n_poly, LANES), 1)
+    mixes = []
     for exposure in range(exp_dev):
-        value = bad_mask[exposure].astype(jnp.float32) / variance[exposure]
-        weight[exposure] = value
-        weight_out[exposure] = value.astype(jnp.bfloat16)
-
-    kernel_rows[...] = jnp.zeros(kernel_rows.shape, jnp.float32)
-
-    def sum_kernels(exposure, carry):
-        sums = [jnp.zeros((ks, ks), jnp.float32) for _ in range(n_poly)]
+        coefs = coefficients[:, exposure, :]
+        mix = jnp.zeros((n_poly, LANES), jnp.float32)
         for j in range(n_sel):
-            image = basis[basis_index[exposure, j]]
-            for p in range(n_poly):
-                sums[p] = sums[p] + coefficients[exposure, j, p] * image
-        for p in range(n_poly):
-            kernel_rows[exposure, p * LANES : p * LANES + ks, 0:ks] = sums[p]
-        return carry
-
-    lax.fori_loop(0, exp_dev, sum_kernels, 0)
+            mix = mix + jnp.where(lane == basis_index[exposure, j], coefs[:, j : j + 1], 0.0)
+        mixes.append(mix)
+        if n_poly < 8:
+            mixes.append(jnp.zeros((8 - n_poly, LANES), jnp.float32))
+    mixes = jnp.concatenate(mixes, axis=0)
+
+    n_pairs = (ks + 1) // 2
+    rows_all = pairs.shape[0] // exp_dev
+    turned_basis[...] = jnp.zeros(turned_basis.shape, jnp.float32)
+    loads[0].wait()
+    for b in range(ks):
+        turned_basis[b * SLOT : b * SLOT + ks, 0:n_basis] = basis[:, b, :]
+
+    for q in range(0, n_pairs, 2):
+        some = lax.dot_general(
+            mixes,
+            turned_basis[q * LANES : (q + 2) * LANES, :],
+            (((1,), (1,)), ((), ())),
+            precision=lax.Precision.HIGHEST,
+            preferred_element_type=jnp.float32,
+        )
+        some = some.astype(jnp.bfloat16).astype(jnp.float32)
+        for half in range(2):
+            for exposure in range(exp_dev):
+                at = exposure * rows_all + (q + half) * n_poly
+                pairs[at : at + n_poly, :] = some[
+                    exposure * 8 : exposure * 8 + n_poly, half * LANES : (half + 1) * LANES
+                ]
+
+    loads[1].wait()
+    loads[2].wait()
+    for exposure in range(exp_dev):
+        weight[exposure] = bad_mask[exposure].astype(jnp.float32) / variance[exposure]
 
     partners = n_epoch
     if n_strip > 1:
@@ -202,32 +243,17 @@
         )
 
     for step in range(1, n_epoch):
-        back(0, weight_out, weight_in, step, False).start()
-
-    n_pairs = (ks + 1) // 2
-    rows_all = pairs.shape[0]
-    row = lax.broadcasted_iota(jnp.int32, (32, LANES), 0)
-    col = lax.broadcasted_iota(jnp.int32, (32, LANES), 1)
-    pick = jnp.where(row < 16, 2 * row, 2 * (row - 16) + 1)
-    pick = (pick == col).astype(jnp.bfloat16)
+        back(0, weight, weight_in, step, False).start()
 
     def build(exposure, carry):
-        rows = kernel_rows[exposure].astype(jnp.bfloat16)
-        turned = lax.dot_general(
-            pick, rows, (((1,), (1,)), ((), ())), preferred_element_type=jnp.float32
-        )
-        for p in range(n_poly):
-            block = turned[:, p * LANES : (p + 1) * LANES]
-            both = block[:16] + pltpu.roll(block[16:], SLOT, 1)
-            pairs[p * n_pairs : (p + 1) * n_pairs, :] = both[:n_pairs]
-        shift = offsets[exposure, 0] + (SHIFT + EDGE_ROWS - RIM)
-        every = pairs[...]
+        shift = offsets[0, exposure] + (SHIFT + EDGE_ROWS - RIM)
+        every = pairs[pl.ds(pl.multiple_of(exposure * rows_all, 8), rows_all), :]
         for y in range(height):
             turns[y * rows_all : (y + 1) * rows_all, :] = pltpu.roll(every, shift + y, 1)
         for p in range(0, n_poly, 2):
             for q in range(n_pairs):
                 halves = [
-                    turns[pl.ds((p + h) * n_pairs + q, height, stride=rows_all), :]
+                    turns[pl.ds(q * n_poly + p + h, height, stride=rows_all), :]
                     for h in range(2)
                 ]
                 toeplitz[
@@ -253,6 +279,7 @@
                 lambda ds=ds, db=db: piece(step, ds, db, True).wait_recv(),
             )
 
+    loads[3].wait()
     for step in range(n_epoch):
         k = lax.rem(me + step, n_epoch)
         arrive(step)
@@ -266,7 +293,7 @@
             axis=0,
         )
         total = width + 2 * LANES
-        slab = pltpu.roll(slab, total - (LANES - RIM + SHIFT) - offsets[k, 1], 1)
+        slab = pltpu.roll(slab, total - (LANES - RIM + SHIFT) - offsets[1, k], 1)
         slab = slab[:, : width + LANES].astype(jnp.bfloat16)
         conv = jnp.zeros((n_poly * height, width), jnp.float32)
         for first in range(0, ks, 4):
@@ -281,11 +308,12 @@
         model = q[0] + r * (q[1] + r * q[3] + c * q[4]) + c * (q[2] + c * q[5])
         left = science[k] - model
         residual[k] = left
+        pltpu.make_async_copy(residual.at[k], residual_out.at[k], local_sem.at[4 + k]).start()
         value = weight[k] * left
         if step == 0:
             own_value[...] = value
         else:
-            value_out[k] = value.astype(jnp.bfloat16)
+            value_out[k] = value
             back(1, value_out, value_in, step, False).start()
 
     numer = [None] * tile_dev
@@ -296,16 +324,18 @@
         if step == 0:
             upper, under = own_value[...], weight[me]
         else:
-            back(0, weight_out, weight_in, step, True).wait_recv()
+            back(0, weight, weight_in, step, True).wait_recv()
             back(1, value_out, value_in, step, True).wait_recv()
-            upper = value_in[k].astype(jnp.float32)
-            under = weight_in[k].astype(jnp.float32)
+            upper = value_in[k]
+            under = weight_in[k]
         for t in range(tile_dev):
             here = (tile == t).astype(jnp.float32)
             numer[t] = upper * here if step == 0 else numer[t] + upper * here
             denom[t] = under * here if step == 0 else denom[t] + under * here
     for t in range(tile_dev):
         coadd[t] = numer[t] / (denom[t] + 1.0)
+    last = pltpu.make_async_copy(coadd, coadd_out, local_sem.at[4 + n_epoch])
+    last.start()
 
     for step in range(n_epoch):
         for ds, db in STEPS:
@@ -316,8 +346,11 @@
                 lambda step=step, ds=ds, db=db: piece(step, ds, db, False).wait_send(),
             )
         if step > 0:
-            back(0, weight_out, weight_in, step, False).wait_send()
+            back(0, weight, weight_in, step, False).wait_send()
             back(1, value_out, value_in, step, False).wait_send()
+        k = lax.rem(me + step, n_epoch)
+        pltpu.make_async_copy(residual.at[k], residual_out.at[k], local_sem.at[4 + k]).wait()
+    last.wait()
 
 
 def local(sizes, template, science, variance, bad_mask, intersection, offsets, basis_index, coefficients, basis):
@@ -332,32 +365,42 @@
     rows_all = -(-n_poly * n_pairs // 8) * 8
     smem = pl.BlockSpec(memory_space=pltpu.SMEM)
     vmem = pl.BlockSpec(memory_space=pltpu.VMEM)
+    free = pl.BlockSpec(memory_space=pl.ANY)
     bf16, f32 = jnp.bfloat16, jnp.float32
     dma = pltpu.SemaphoreType.DMA
+    offsets = offsets.T
+    coefficients = coefficients.transpose(2, 0, 1)
+    basis = basis.transpose(1, 2, 0)
     return pl.pallas_call(
         functools.partial(kernel, sizes),
         out_shape=(
             jax.ShapeDtypeStruct(science.shape, f32),
             jax.ShapeDtypeStruct(template.shape, f32),
         ),
-        in_specs=[smem] * 4 + [vmem] * 5,
-        out_specs=(vmem, vmem),
+        in_specs=[smem] * 3 + [vmem] * 2 + [free] * 4,
+        out_specs=(free, free),
         scratch_shapes=[
+            pltpu.VMEM(science.shape, f32),
+            pltpu.VMEM(science.shape, f32),
+            pltpu.VMEM(science.shape, jnp.int32),
+            pltpu.VMEM(basis.shape, f32),
+            pltpu.VMEM(science.shape, f32),
+            pltpu.VMEM(template.shape, f32),
             pltpu.VMEM((n_epoch, height, width), bf16),
             pltpu.VMEM((n_epoch, EDGE_ROWS, width), bf16),
             pltpu.VMEM((exp_dev, height, lanes_all), bf16),
             pltpu.VMEM((exp_dev, EDGE_ROWS, lanes_all), bf16),
             pltpu.VMEM((exp_dev, EDGE_ROWS, lanes_all), bf16),
-            pltpu.VMEM((exp_dev, n_poly * LANES, LANES), f32),
-            pltpu.VMEM((rows_all, LANES), f32),
+            pltpu.VMEM((n_pairs * LANES, LANES), f32),
+            pltpu.VMEM((exp_dev * rows_all, LANES), f32),
             pltpu.VMEM((height * rows_all, LANES), f32),
             pltpu.VMEM((exp_dev, n_poly * height, n_pairs * LANES), bf16),
             pltpu.VMEM((exp_dev, height, width), f32),
-            pltpu.VMEM((exp_dev, height, width), bf16),
-            pltpu.VMEM((exp_dev, height, width), bf16),
-            pltpu.VMEM((exp_dev, height, width), bf16),
-            pltpu.VMEM((exp_dev, height, width), bf16),
+            pltpu.VMEM((exp_dev, height, width), f32),
+            pltpu.VMEM((exp_dev, height, width), f32),
+            pltpu.VMEM((exp_dev, height, width), f32),
             pltpu.VMEM((height, width), f32),
+            dma((5 + n_epoch,)),
             dma((n_epoch, 3, 3)),
             dma((n_epoch, 3, 3)),
             dma((2, n_epoch)),

time: 26.5 us -> 21.4 us (0.81)
  local copies, waits for them, and re-layouts: 7 us -> 2.18 us
    unnamed x7 -> x4, local copies, waits for them, and re-layouts: 7 us -> 2.18 us
where the time goes in v2:
time: 21.4 us; the launch traced here: 21.1 us
  Pallas kernels  18.3 us (86%)
  local copies, waits for them, and re-layouts  2.18 us (10%)
  between operations  0.65 us (3%)
    pallas_call x1, Pallas kernels, local(): pl.pallas_call(functools.partial(kernel, sizes), out_shape=(jax.ShapeDtyp...  18.3 us
    unnamed x4, local copies, waits for them, and re-layouts  2.18 us

profile of v2, /device:TPU:0, one launch (start us, length us, event | category | flops | bytes accessed | tf_op | source)
XLA Modules:
  0.0 21.1 jit_solution(1877630634506530205)
XLA Ops:
  0.6 18.3 %shard_map.104 = (f32[4,24,256]{2,1,0:T(8,128)}, f32[2,24,256]{2,1,0:T(8,128)}) custom-call(s32[16]{0:T(128)} %intersection.1, s32[2,4]{1,0:T(2,128)} %bitcast.5, s32[4,16]{1,0:T(4,128)} %basis_index.1, f32[6,4,16]{2,1,0:T(4,128)} %bitcast.4, bf16[2,24,256]{2,1,0:T(8,128)(2,1)} %template.1, f32[4,24,256]{2,1,0:T(8,128)} %science_hbm.1, ...), custom_call_target="tpu_custom_call" | custom-call | tf_op jit(solution)/shard_map/pallas_call | solution.py:374
  19.0 0.0 copy-start
  19.0 1.6 %copy.13 = f32[4,24,256]{2,1,0:T(8,128)} copy(f32[4,24,256]{2,1,0:T(8,128)} %get-tuple-element.4) | data formatting | bytes 196608
  20.5 0.0 copy-done
  20.5 0.6 %copy.14 = f32[2,24,256]{2,1,0:T(8,128)} copy(f32[2,24,256]{2,1,0:T(8,128)S(1)} %copy-done) | data formatting | bytes 98304
Async XLA Ops:
  19.0 1.6 %copy-start = (f32[2,24,256]{2,1,0:T(8,128)S(1)}, f32[2,24,256]{2,1,0:T(8,128)}, u32[]{:S(2)}) copy-start(f32[2,24,256]{2,1,0:T(8,128)} %get-tuple-element.5) | copy-start | bytes 147460

commit v3 on v2

--- a/solution.py
+++ b/solution.py
@@ -20,17 +20,22 @@
 
 def kernel(
     sizes,
-    intersection,
-    offsets,
-    basis_index,
-    coefficients,
-    template,
+    intersection_hbm,
+    offsets_hbm,
+    basis_index_hbm,
+    coefficients_hbm,
+    template_hbm,
     science_hbm,
     variance_hbm,
     bad_mask_hbm,
     basis_hbm,
     residual_out,
     coadd_out,
+    intersection,
+    offsets,
+    basis_index,
+    coefficients,
+    template,
     science,
     variance,
     bad_mask,
@@ -67,6 +72,11 @@
     strip = lax.axis_index("strip")
     band = lax.axis_index("band")
 
+    side = 2 * lax.div(2 * me, n_epoch) - 1
+
+    def away(step):
+        return lax.rem(me + n_epoch + side * step, n_epoch)
+
     def target(epoch, ds, db):
         return (group, epoch, strip + ds, band + db)
 
@@ -90,20 +100,6 @@
         else:
             pl.when(jnp.logical_and(sides[0], sides[1]))(body)
 
-    barrier = pltpu.get_barrier_semaphore()
-    for ds, db in STEPS:
-
-        def greet(ds=ds, db=db):
-            for step in range(n_epoch):
-                if step == 0 and ds == 0 and db == 0:
-                    continue
-                epoch = lax.rem(me + step, n_epoch)
-                pl.semaphore_signal(
-                    barrier, inc=1, device_id=target(epoch, ds, db), device_id_type=MESH
-                )
-
-        guarded(there(ds, db), greet)
-
     loads = [
         pltpu.make_async_copy(held, here, local_sem.at[i])
         for i, (held, here) in enumerate(
@@ -112,14 +108,35 @@
                 (variance_hbm, variance),
                 (bad_mask_hbm, bad_mask),
                 (science_hbm, science),
+                (intersection_hbm, intersection),
+                (template_hbm, template),
+                (basis_index_hbm, basis_index),
+                (coefficients_hbm, coefficients),
+                (offsets_hbm, offsets),
             )
         )
     ]
-    for load in loads:
-        load.start()
-
+    for i in (4, 5, 6, 7, 0, 1, 2, 3, 8):
+        loads[i].start()
+
+    barrier = pltpu.get_barrier_semaphore()
+    for ds, db in STEPS:
+
+        def greet(ds=ds, db=db):
+            for step in range(n_epoch):
+                if step == 0 and ds == 0 and db == 0:
+                    continue
+                epoch = away(step)
+                pl.semaphore_signal(
+                    barrier, inc=1, device_id=target(epoch, ds, db), device_id_type=MESH
+                )
+
+        guarded(there(ds, db), greet)
+
+    loads[4].wait()
+    loads[5].wait()
     for step in range(n_epoch):
-        epoch = lax.rem(me + step, n_epoch)
+        epoch = away(step)
         tile = intersection[epoch * exp_dev + me] - me * tile_dev
         chosen = template[jnp.clip(tile, 0, tile_dev - 1)]
         full[epoch] = chosen
@@ -151,6 +168,8 @@
             def _():
                 low[:, :, lanes] = jnp.full(low[:, :, lanes].shape, zero)
 
+    loads[6].wait()
+    loads[7].wait()
     lane = lax.broadcasted_iota(jnp.int32, (n_poly, LANES), 1)
     mixes = []
     for exposure in range(exp_dev):
@@ -201,7 +220,7 @@
     pl.semaphore_wait(barrier, partners - 1)
 
     def piece(step, ds, db, arriving):
-        other = lax.rem(me + step, n_epoch)
+        other = away(step)
         held = {0: slice(0, width), 1: slice(width - LANES, width), -1: slice(0, LANES)}[db]
         lands = {
             0: slice(LANES, LANES + width),
@@ -231,7 +250,7 @@
             guarded(there(ds, db), lambda step=step, ds=ds, db=db: piece(step, ds, db, False).start())
 
     def back(which, out, into, step, arriving):
-        other = lax.rem(me + step, n_epoch)
+        other = away(step)
         slot = other if arriving else me
         return pltpu.make_async_remote_copy(
             src_ref=out.at[other],
@@ -244,6 +263,8 @@
 
     for step in range(1, n_epoch):
         back(0, weight, weight_in, step, False).start()
+
+    loads[8].wait()
 
     def build(exposure, carry):
         shift = offsets[0, exposure] + (SHIFT + EDGE_ROWS - RIM)
@@ -281,7 +302,7 @@
 
     loads[3].wait()
     for step in range(n_epoch):
-        k = lax.rem(me + step, n_epoch)
+        k = away(step)
         arrive(step)
         slab = jnp.concatenate(
             [
@@ -308,7 +329,7 @@
         model = q[0] + r * (q[1] + r * q[3] + c * q[4]) + c * (q[2] + c * q[5])
         left = science[k] - model
         residual[k] = left
-        pltpu.make_async_copy(residual.at[k], residual_out.at[k], local_sem.at[4 + k]).start()
+        pltpu.make_async_copy(residual.at[k], residual_out.at[k], local_sem.at[9 + k]).start()
         value = weight[k] * left
         if step == 0:
             own_value[...] = value
@@ -319,7 +340,7 @@
     numer = [None] * tile_dev
     denom = [None] * tile_dev
     for step in range(n_epoch):
-        k = lax.rem(me + step, n_epoch)
+        k = away(step)
         tile = intersection[k * exp_dev + me] - me * tile_dev
         if step == 0:
             upper, under = own_value[...], weight[me]
@@ -334,7 +355,7 @@
             denom[t] = under * here if step == 0 else denom[t] + under * here
     for t in range(tile_dev):
         coadd[t] = numer[t] / (denom[t] + 1.0)
-    last = pltpu.make_async_copy(coadd, coadd_out, local_sem.at[4 + n_epoch])
+    last = pltpu.make_async_copy(coadd, coadd_out, local_sem.at[9 + n_epoch])
     last.start()
 
     for step in range(n_epoch):
@@ -348,9 +369,27 @@
         if step > 0:
             back(0, weight, weight_in, step, False).wait_send()
             back(1, value_out, value_in, step, False).wait_send()
-        k = lax.rem(me + step, n_epoch)
-        pltpu.make_async_copy(residual.at[k], residual_out.at[k], local_sem.at[4 + k]).wait()
+        k = away(step)
+        pltpu.make_async_copy(residual.at[k], residual_out.at[k], local_sem.at[9 + k]).wait()
     last.wait()
+
+
+def leave(residual, coadd, residual_out, coadd_out, images, tiles, sem):
+    arrive = [
+        pltpu.make_async_copy(residual, images, sem.at[0]),
+        pltpu.make_async_copy(coadd, tiles, sem.at[1]),
+    ]
+    depart = [
+        pltpu.make_async_copy(images, residual_out, sem.at[2]),
+        pltpu.make_async_copy(tiles, coadd_out, sem.at[3]),
+    ]
+    for copy in arrive:
+        copy.start()
+    for i in (1, 0):
+        arrive[i].wait()
+        depart[i].start()
+    for copy in depart:
+        copy.wait()
 
 
 def local(sizes, template, science, variance, bad_mask, intersection, offsets, basis_index, coefficients, basis):
@@ -363,23 +402,27 @@
     lanes_all = width + 2 * LANES
     n_pairs = (ks + 1) // 2
     rows_all = -(-n_poly * n_pairs // 8) * 8
-    smem = pl.BlockSpec(memory_space=pltpu.SMEM)
-    vmem = pl.BlockSpec(memory_space=pltpu.VMEM)
+    far = pl.BlockSpec(memory_space=pltpu.HBM)
     free = pl.BlockSpec(memory_space=pl.ANY)
     bf16, f32 = jnp.bfloat16, jnp.float32
     dma = pltpu.SemaphoreType.DMA
     offsets = offsets.T
     coefficients = coefficients.transpose(2, 0, 1)
     basis = basis.transpose(1, 2, 0)
-    return pl.pallas_call(
+    residual, coadd = pl.pallas_call(
         functools.partial(kernel, sizes),
         out_shape=(
             jax.ShapeDtypeStruct(science.shape, f32),
             jax.ShapeDtypeStruct(template.shape, f32),
         ),
-        in_specs=[smem] * 3 + [vmem] * 2 + [free] * 4,
+        in_specs=[far] * 9,
         out_specs=(free, free),
         scratch_shapes=[
+            pltpu.SMEM(intersection.shape, jnp.int32),
+            pltpu.SMEM(offsets.shape, jnp.int32),
+            pltpu.SMEM(basis_index.shape, jnp.int32),
+            pltpu.VMEM(coefficients.shape, f32),
+            pltpu.VMEM(template.shape, bf16),
             pltpu.VMEM(science.shape, f32),
             pltpu.VMEM(science.shape, f32),
             pltpu.VMEM(science.shape, jnp.int32),
@@ -400,17 +443,33 @@
             pltpu.VMEM((exp_dev, height, width), f32),
             pltpu.VMEM((exp_dev, height, width), f32),
             pltpu.VMEM((height, width), f32),
-            dma((5 + n_epoch,)),
+            dma((10 + n_epoch,)),
             dma((n_epoch, 3, 3)),
             dma((n_epoch, 3, 3)),
             dma((2, n_epoch)),
             dma((2, n_epoch)),
         ],
-        compiler_params=pltpu.CompilerParams(collective_id=0, has_side_effects=True),
+        compiler_params=pltpu.CompilerParams(
+            collective_id=0, has_side_effects=True
+        ),
     )(
         intersection, offsets, basis_index, coefficients,
         template, science, variance, bad_mask, basis,
     )
+    return pl.pallas_call(
+        leave,
+        out_shape=(
+            jax.ShapeDtypeStruct(science.shape, f32),
+            jax.ShapeDtypeStruct(template.shape, f32),
+        ),
+        in_specs=[free] * 2,
+        out_specs=(free, free),
+        scratch_shapes=[
+            pltpu.VMEM(science.shape, f32),
+            pltpu.VMEM(template.shape, f32),
+            dma((4,)),
+        ],
+    )(residual, coadd)
 
 
 def solution(mesh):

time: 21.4 us -> 19.6 us (0.916)
  local copies, waits for them, and re-layouts: 2.18 us -> 0 us
  Pallas kernels: 18.3 us -> 18.8 us
    unnamed x4 -> x0, local copies, waits for them, and re-layouts: 2.18 us -> none
    pallas_call x0 -> x1, Pallas kernels: none -> 1.57 us  [local(): pl.pallas_call(leave, out_shape=(jax.ShapeDtypeStruct(science.shape, f32)...]
    pallas_call x1, Pallas kernels: 18.3 us -> 17.2 us  [local(): pl.pallas_call(functools.partial(kernel, sizes), out_shape=(jax.ShapeDtyp...]
where the time goes in v3:
time: 19.6 us; the launch traced here: 19.5 us
  Pallas kernels  18.8 us (96%)
  between operations  0.64 us (3%)
    pallas_call x1, Pallas kernels, local(): pl.pallas_call(functools.partial(kernel, sizes), out_shape=(jax.ShapeDtyp...  17.2 us
    pallas_call x1, Pallas kernels, local(): pl.pallas_call(leave, out_shape=(jax.ShapeDtypeStruct(science.shape, f32)...  1.57 us

profile of v3, /device:TPU:0, one launch (start us, length us, event | category | flops | bytes accessed | tf_op | source)
XLA Modules:
  0.0 19.5 jit_solution(1313173744879441640)
XLA Ops:
  0.6 17.2 %shard_map.104 = (f32[4,24,256]{2,1,0:T(8,128)}, f32[2,24,256]{2,1,0:T(8,128)}) custom-call(s32[16]{0:T(128)} %intersection_hbm.1, s32[2,4]{1,0:T(2,128)} %bitcast.5, s32[4,16]{1,0:T(4,128)} %basis_index_hbm.1, f32[6,4,16]{2,1,0:T(4,128)} %bitcast.4, bf16[2,24,256]{2,1,0:T(8,128)(2,1)} %template_hbm.1, f32[4,24,256]{2,1,0:T(8,128)} %science_hbm.1, ...), custom_call_target="tpu_custom_call" | custom-call | tf_op jit(solution)/shard_map/pallas_call | solution.py:412
  17.9 1.6 %shard_map.105 = (f32[4,24,256]{2,1,0:T(8,128)}, f32[2,24,256]{2,1,0:T(8,128)}) custom-call(f32[4,24,256]{2,1,0:T(8,128)} %get-tuple-element.4.residual, f32[2,24,256]{2,1,0:T(8,128)} %get-tuple-element.5.coadd), custom_call_target="tpu_custom_call" | custom-call | tf_op jit(solution)/shard_map/pallas_call | solution.py:459

commit v4 on v3

--- a/solution.py
+++ b/solution.py
@@ -168,48 +168,6 @@
             def _():
                 low[:, :, lanes] = jnp.full(low[:, :, lanes].shape, zero)
 
-    loads[6].wait()
-    loads[7].wait()
-    lane = lax.broadcasted_iota(jnp.int32, (n_poly, LANES), 1)
-    mixes = []
-    for exposure in range(exp_dev):
-        coefs = coefficients[:, exposure, :]
-        mix = jnp.zeros((n_poly, LANES), jnp.float32)
-        for j in range(n_sel):
-            mix = mix + jnp.where(lane == basis_index[exposure, j], coefs[:, j : j + 1], 0.0)
-        mixes.append(mix)
-        if n_poly < 8:
-            mixes.append(jnp.zeros((8 - n_poly, LANES), jnp.float32))
-    mixes = jnp.concatenate(mixes, axis=0)
-
-    n_pairs = (ks + 1) // 2
-    rows_all = pairs.shape[0] // exp_dev
-    turned_basis[...] = jnp.zeros(turned_basis.shape, jnp.float32)
-    loads[0].wait()
-    for b in range(ks):
-        turned_basis[b * SLOT : b * SLOT + ks, 0:n_basis] = basis[:, b, :]
-
-    for q in range(0, n_pairs, 2):
-        some = lax.dot_general(
-            mixes,
-            turned_basis[q * LANES : (q + 2) * LANES, :],
-            (((1,), (1,)), ((), ())),
-            precision=lax.Precision.HIGHEST,
-            preferred_element_type=jnp.float32,
-        )
-        some = some.astype(jnp.bfloat16).astype(jnp.float32)
-        for half in range(2):
-            for exposure in range(exp_dev):
-                at = exposure * rows_all + (q + half) * n_poly
-                pairs[at : at + n_poly, :] = some[
-                    exposure * 8 : exposure * 8 + n_poly, half * LANES : (half + 1) * LANES
-                ]
-
-    loads[1].wait()
-    loads[2].wait()
-    for exposure in range(exp_dev):
-        weight[exposure] = bad_mask[exposure].astype(jnp.float32) / variance[exposure]
-
     partners = n_epoch
     if n_strip > 1:
         near = jnp.minimum(strip, 1) + jnp.minimum(n_strip - 1 - strip, 1)
@@ -260,6 +218,48 @@
             device_id=target(other, 0, 0),
             device_id_type=MESH,
         )
+
+    loads[1].wait()
+    loads[2].wait()
+    for exposure in range(exp_dev):
+        weight[exposure] = bad_mask[exposure].astype(jnp.float32) / variance[exposure]
+
+    loads[6].wait()
+    loads[7].wait()
+    lane = lax.broadcasted_iota(jnp.int32, (n_poly, LANES), 1)
+    mixes = []
+    for exposure in range(exp_dev):
+        coefs = coefficients[:, exposure, :]
+        mix = jnp.zeros((n_poly, LANES), jnp.float32)
+        for j in range(n_sel):
+            mix = mix + jnp.where(lane == basis_index[exposure, j], coefs[:, j : j + 1], 0.0)
+        mixes.append(mix)
+        if n_poly < 8:
+            mixes.append(jnp.zeros((8 - n_poly, LANES), jnp.float32))
+    mixes = jnp.concatenate(mixes, axis=0)
+
+    n_pairs = (ks + 1) // 2
+    rows_all = pairs.shape[0] // exp_dev
+    turned_basis[...] = jnp.zeros(turned_basis.shape, jnp.float32)
+    loads[0].wait()
+    for b in range(ks):
+        turned_basis[b * SLOT : b * SLOT + ks, 0:n_basis] = basis[:, b, :]
+
+    for q in range(0, n_pairs, 2):
+        some = lax.dot_general(
+            mixes,
+            turned_basis[q * LANES : (q + 2) * LANES, :],
+            (((1,), (1,)), ((), ())),
+            precision=lax.Precision.HIGHEST,
+            preferred_element_type=jnp.float32,
+        )
+        some = some.astype(jnp.bfloat16).astype(jnp.float32)
+        for half in range(2):
+            for exposure in range(exp_dev):
+                at = exposure * rows_all + (q + half) * n_poly
+                pairs[at : at + n_poly, :] = some[
+                    exposure * 8 : exposure * 8 + n_poly, half * LANES : (half + 1) * LANES
+                ]
 
     for step in range(1, n_epoch):
         back(0, weight, weight_in, step, False).start()
@@ -375,17 +375,20 @@
 
 
 def leave(residual, coadd, residual_out, coadd_out, images, tiles, sem):
+    parts = [
+        (held.at[i], here.at[i], out.at[i])
+        for held, here, out in ((residual, images, residual_out), (coadd, tiles, coadd_out))
+        for i in range(here.shape[0])
+    ]
     arrive = [
-        pltpu.make_async_copy(residual, images, sem.at[0]),
-        pltpu.make_async_copy(coadd, tiles, sem.at[1]),
+        pltpu.make_async_copy(held, here, sem.at[0, i]) for i, (held, here, _) in enumerate(parts)
     ]
     depart = [
-        pltpu.make_async_copy(images, residual_out, sem.at[2]),
-        pltpu.make_async_copy(tiles, coadd_out, sem.at[3]),
+        pltpu.make_async_copy(here, out, sem.at[1, i]) for i, (_, here, out) in enumerate(parts)
     ]
     for copy in arrive:
         copy.start()
-    for i in (1, 0):
+    for i in range(len(parts)):
         arrive[i].wait()
         depart[i].start()
     for copy in depart:
@@ -467,7 +470,7 @@
         scratch_shapes=[
             pltpu.VMEM(science.shape, f32),
             pltpu.VMEM(template.shape, f32),
-            dma((4,)),
+            dma((2, exp_dev + tile_dev)),
         ],
     )(residual, coadd)
 

time: 19.6 us -> 19.5 us (level)
  no operation moved by 1% of the time
where the time goes in v4:
time: 19.5 us; the launch traced here: 19.3 us
  Pallas kernels  18.7 us (96%)
  between operations  0.64 us (3%)
    pallas_call x1, Pallas kernels, local(): pl.pallas_call(functools.partial(kernel, sizes), out_shape=(jax.ShapeDtyp...  17.1 us
    pallas_call x1, Pallas kernels, local(): pl.pallas_call(leave, out_shape=(jax.ShapeDtypeStruct(science.shape, f32)...  1.54 us

profile of v4, /device:TPU:0, one launch (start us, length us, event | category | flops | bytes accessed | tf_op | source)
XLA Modules:
  0.0 19.3 jit_solution(106455296077303238)
XLA Ops:
  0.6 17.1 %shard_map.104 = (f32[4,24,256]{2,1,0:T(8,128)}, f32[2,24,256]{2,1,0:T(8,128)}) custom-call(s32[16]{0:T(128)} %intersection_hbm.1, s32[2,4]{1,0:T(2,128)} %bitcast.5, s32[4,16]{1,0:T(4,128)} %basis_index_hbm.1, f32[6,4,16]{2,1,0:T(4,128)} %bitcast.4, bf16[2,24,256]{2,1,0:T(8,128)(2,1)} %template_hbm.1, f32[4,24,256]{2,1,0:T(8,128)} %science_hbm.1, ...), custom_call_target="tpu_custom_call" | custom-call | tf_op jit(solution)/shard_map/pallas_call | solution.py:415
  17.8 1.5 %shard_map.105 = (f32[4,24,256]{2,1,0:T(8,128)}, f32[2,24,256]{2,1,0:T(8,128)}) custom-call(f32[4,24,256]{2,1,0:T(8,128)} %get-tuple-element.4.residual, f32[2,24,256]{2,1,0:T(8,128)} %get-tuple-element.5.coadd), custom_call_target="tpu_custom_call" | custom-call | tf_op jit(solution)/shard_map/pallas_call | solution.py:462

commit v5 on v4

--- a/solution.py
+++ b/solution.py
@@ -15,7 +15,7 @@
 SLOT = 64
 
 MESH = pl.DeviceIdType.MESH
-STEPS = [(ds, db) for ds in (0, -1, 1) for db in (0, -1, 1)]
+STEPS = [(ds, db) for ds in (-1, 1, 0) for db in (-1, 1, 0)]
 
 
 def kernel(

time: 19.5 us -> 19.3 us (0.990)
  Pallas kernels: 18.7 us -> 18.5 us
where the time goes in v5:
time: 19.3 us; the launch traced here: 19.1 us
  Pallas kernels  18.5 us (96%)
  between operations  0.64 us (3%)
    pallas_call x1, Pallas kernels, local(): pl.pallas_call(functools.partial(kernel, sizes), out_shape=(jax.ShapeDtyp...  17 us
    pallas_call x1, Pallas kernels, local(): pl.pallas_call(leave, out_shape=(jax.ShapeDtypeStruct(science.shape, f32)...  1.54 us

profile of v5, /device:TPU:0, one launch (start us, length us, event | category | flops | bytes accessed | tf_op | source)
XLA Modules:
  0.0 19.1 jit_solution(13232621029422435990)
XLA Ops:
  0.6 17.0 %shard_map.104 = (f32[4,24,256]{2,1,0:T(8,128)}, f32[2,24,256]{2,1,0:T(8,128)}) custom-call(s32[16]{0:T(128)} %intersection_hbm.1, s32[2,4]{1,0:T(2,128)} %bitcast.5, s32[4,16]{1,0:T(4,128)} %basis_index_hbm.1, f32[6,4,16]{2,1,0:T(4,128)} %bitcast.4, bf16[2,24,256]{2,1,0:T(8,128)(2,1)} %template_hbm.1, f32[4,24,256]{2,1,0:T(8,128)} %science_hbm.1, ...), custom_call_target="tpu_custom_call" | custom-call | tf_op jit(solution)/shard_map/pallas_call | solution.py:415
  17.6 1.5 %shard_map.105 = (f32[4,24,256]{2,1,0:T(8,128)}, f32[2,24,256]{2,1,0:T(8,128)}) custom-call(f32[4,24,256]{2,1,0:T(8,128)} %get-tuple-element.4.residual, f32[2,24,256]{2,1,0:T(8,128)} %get-tuple-element.5.coadd), custom_call_target="tpu_custom_call" | custom-call | tf_op jit(solution)/shard_map/pallas_call | solution.py:462
